TPU v7x, 256 devices: a whole 4x4x8 slice. The times are simulated.
256 devices in a mesh: dp: 4 (over x), tensor: 64 (over y, z, core).
Axes of the slice: x: 4, y: 4, z: 8, core: 2. Of those that a mesh axis runs over, the one named last changes fastest.
Arguments:
- grad_out: bfloat16 [4096, 8192], P('dp', 'tensor'), may hold values from -6 to 6
- acts: bfloat16 [4096, 16384], P('dp', 'tensor'), may hold values from -6 to 6
- weight: bfloat16 [8192, 16384], P('tensor'), may hold values from -0.078125 to 0.078125
- block_mask: int32 [64, 128], replicated, may hold values from 0 to 1, as said below
Outputs:
- grad_acts: bfloat16 [4096, 16384], P('dp', 'tensor')
- grad_weight: float32 [8192, 16384], P(('dp', 'tensor'))
Inputs may be any that keep to these rules, and one draw needn't show every extreme that they name: `block_mask`: kept shares differ between groups of 2 consecutive block columns, from about three twentieths to nine twentieths.
All inputs are finite; a program needn't handle non-finite values.
Results may differ from a plain program's by a relative error of at most 0.001.
Values may be sent and summed in bfloat16 or wider, within the bound.
A program may use at most 128 MiB of HBM per device.

v0:
```python
import jax
import jax.numpy as jnp
from jax import lax
from jax.sharding import PartitionSpec as P


def expand_mask(mask, side):
    rows, cols = mask.shape
    full = jnp.broadcast_to(mask[:, None, :, None], (rows, side, cols, side))
    return full.reshape(rows * side, cols * side)


def body(grad_out, acts, weight, block_mask):
    tensor_count = lax.axis_size("tensor")
    group_count = lax.axis_size("dp")
    position = lax.axis_index("tensor")
    d_tile = weight.shape[0]
    full_width = weight.shape[1]
    ff_tile = acts.shape[1]
    side = full_width // block_mask.shape[1]
    total_rows = d_tile * tensor_count
    row_mask = lax.dynamic_slice_in_dim(block_mask, position * (d_tile // side), d_tile // side, 0)
    kept = weight * expand_mask(row_mask, side).astype(jnp.bfloat16)
    columns = lax.all_to_all(kept, "tensor", split_axis=1, concat_axis=0, tiled=True)
    piece = lax.all_gather(grad_out, "tensor", axis=1, tiled=True)
    input_grad = jnp.dot(piece, columns, preferred_element_type=jnp.float32)
    grad_rows = lax.dot_general(
        piece, acts, (((0,), (0,)), ((), ())), preferred_element_type=jnp.float32
    )
    weight_grad = grad_rows
    input_grad, weight_grad = (input_grad, weight_grad)
    grad_acts = input_grad.astype(jnp.bfloat16)
    col_mask = lax.dynamic_slice_in_dim(
        block_mask, position * (ff_tile // side), ff_tile // side, 1
    )
    scale_factor = 1.0 / (grad_out.shape[0] * group_count) ** 0.5
    weight_grad = weight_grad * expand_mask(col_mask, side).astype(jnp.float32) * scale_factor
    quarter = total_rows // (group_count * tensor_count)
    reordered = weight_grad.reshape(group_count, tensor_count, quarter, ff_tile)
    reordered = jnp.transpose(reordered, (1, 0, 2, 3)).reshape(total_rows, ff_tile)
    owned = lax.all_to_all(reordered, "tensor", split_axis=0, concat_axis=1, tiled=True)
    grad_weight = lax.psum_scatter(owned, "dp", scatter_dimension=0, tiled=True)
    return (grad_acts, grad_weight)


def solution(mesh):
    in_specs = (P("dp", "tensor"), P("dp", "tensor"), P("tensor", None), P())
    out_specs = (P("dp", "tensor"), P(("dp", "tensor"), None))
    return jax.shard_map(body, mesh=mesh, in_specs=in_specs, out_specs=out_specs, check_vma=False)
```

profile of v0, /device:TPU:1, one launch (start us, length us, event | category | flops | bytes accessed | tf_op | source)
XLA Modules:
  0.0 497.6 jit_solution(10132291511642374837)
XLA Ops:
  7.2 0.0 copy-start
  7.2 0.0 all-gather.2.cloned.1.call-start
  7.2 0.7 all-gather.2.cloned.1.call-update
  7.9 0.0 reduce-scatter.4.cloned.1.call-start
  8.0 0.8 dynamic-slice_convert_fusion
  8.8 113.1 %all-gather.2.cloned.1.call-done = bf16[1024,8192]{1,0:T(8,128)(2,1)} async-done(((bf16[1024,128]{1,0:T(8,128)(2,1)}), bf16[1024,8192]{1,0:T(8,128)(2,1)}) %all-gather.2.cloned.1.call-update) | async-done | bytes 16777232 | tf_op jit(solution)/shard_map/all_gather | solution.py:25
  121.9 5.5 %broadcast_in_dim.16 = f32[64,128,2,128]{3,2,1,0:T(2,128)} broadcast(f32[64,2]{1,0:T(8,128)S(1)} %dynamic-slice_convert_fusion), dimensions={0,2} | broadcast | bytes 8389120 | tf_op jit(solution)/shard_map/broadcast_in_dim | solution.py:9
  127.4 0.0 copy-done
  127.4 13.7 %fusion = f32[8192,256]{1,0:T(8,128)S(1)} fusion(bf16[1024,8192]{1,0:T(8,128)(2,1)} %all-gather.2.cloned.1.call-done, bf16[1024,256]{1,0:T(8,128)(2,1)S(1)} %copy-done, f32[1024,8,2,128]{3,2,1,0:T(2,128)} %bitcast.29), kind=kOutput, calls=%fused_computation.1 | convolution fusion | flops 4299161600 | bytes 34078720 | tf_op jit(solution)/shard_map/dot_general | solution.py:27
  141.1 1.7 copy.17
  142.7 192.2 %all_to_all.38 = f32[64,128,256]{2,1,0:T(8,128)} all-to-all(f32[64,128,256]{2,1,0:T(8,128)S(1)} %bitcast.24), channel_id=1, replica_groups=mesh['dp'=4,'tensor'=64] {'tensor'}, dimensions={0} | all-to-all | bytes 16777216 | tf_op jit(solution)/shard_map/all_to_all | solution.py:41
  334.9 9.0 %copy.18 = f32[128,64,256]{0,2,1:T(8,128)} copy(f32[128,64,256]{2,0,1:T(8,128)} %bitcast.25) | data formatting | bytes 16777216 | tf_op jit(solution)/shard_map/all_to_all | solution.py:41
  343.9 9.0 %copy.21 = f32[128,16384]{1,0:T(8,128)} copy(f32[128,16384]{0,1:T(8,128)} %bitcast.26) | data formatting | bytes 16777216
  352.8 0.0 reduce-scatter.4.cloned.1.call-update
  352.9 6.4 %copy.15 = bf16[128,16384]{0,1:T(8,128)(2,1)} copy(bf16[128,16384]{1,0:T(8,128)(2,1)} %param.6) | data formatting | bytes 8388608 | tf_op args[2]
  359.2 0.7 convert_bitcast_fusion
  359.9 0.1 broadcast_bitcast_fusion
  360.0 10.0 %broadcast_multiply_fusion = bf16[128,16384]{0,1:T(8,128)(2,1)S(1)} fusion(bf16[128,16384]{0,1:T(8,128)(2,1)} %copy.15, bf16[16384]{0:T(1024)(128)(2,1)S(1)} %broadcast_bitcast_fusion), kind=kLoop, calls=%fused_computation.2 | loop fusion | flops 2097152 | bytes 8421376 | tf_op jit(solution)/shard_map/mul | solution.py:23
  370.0 101.7 %all_to_all.39 = bf16[128,64,256]{0,2,1:T(8,128)(2,1)} all-to-all(bf16[128,64,256]{0,2,1:T(8,128)(2,1)S(1)} %bitcast.27), channel_id=1, replica_groups=mesh['dp'=4,'tensor'=64] {'tensor'}, dimensions={1} | all-to-all | bytes 8388608 | tf_op jit(solution)/shard_map/all_to_all | solution.py:24
  471.7 6.4 %copy.16 = bf16[64,128,256]{2,1,0:T(8,128)(2,1)} copy(bf16[64,128,256]{1,2,0:T(8,128)(2,1)} %bitcast.28) | data formatting | bytes 8388608 | tf_op jit(solution)/shard_map/all_to_all | solution.py:24
  478.1 0.0 copy-start.1
  478.1 11.6 %fusion.1 = bf16[1024,256]{0,1:T(8,128)(2,1)S(1)} fusion(bf16[8192,256]{1,0:T(8,128)(2,1)} %bitcast.31, bf16[1024,8192]{1,0:T(8,128)(2,1)} %all-gather.2.cloned.1.call-done), kind=kOutput, calls=%fused_computation.4 | convolution fusion | flops 4295229440 | bytes 21495808 | tf_op jit(solution)/shard_map/dot_general | solution.py:26
  489.8 1.0 copy.19
  490.8 0.0 reduce-scatter.4.cloned.1.call-done
  490.8 0.0 copy-done.1
Async XLA Ops:
  7.2 120.2 %copy-start = (bf16[1024,256]{1,0:T(8,128)(2,1)S(1)}, bf16[1024,256]{1,0:T(8,128)(2,1)}, u32[]{:S(2)}) copy-start(bf16[1024,256]{1,0:T(8,128)(2,1)} %param.5) | copy-start | bytes 1572868
  7.2 114.8 %all-gather.2.cloned.1.call-start = ((), (), s32[]{:S(2)}) async-start(), calls=%async_computation.3 | async-start | bytes 17039360 | tf_op jit(solution)/shard_map/all_gather | solution.py:25
  7.9 482.8 %reduce-scatter.4.cloned.1.call-start = ((), (), s32[]{:S(2)}) async-start(), calls=%async_computation.4 | async-start | bytes 10485760
  478.1 12.7 %copy-start.1 = (bf16[1024,256]{1,0:T(8,128)(2,1)S(1)}, bf16[1024,256]{1,0:T(8,128)(2,1)}, u32[]{:S(2)}) copy-start(bf16[1024,256]{1,0:T(8,128)(2,1)} %param.5) | copy-start | bytes 1572868
Sparse Core Ops, SparseCore 0:
  10.6 111.3 all-gather.1
  353.0 79.4 reduce-scatter.3
where the time goes:
time: 498 us
  blocking collectives  294 us (59%)
  waiting for transfers between devices  114 us (23%)
  local copies, waits for them, and re-layouts  38.9 us (8%)
  matrix products  25.3 us (5%)
  between operations  14.1 us (3%)
  other arithmetic  11.6 us (2%)
    all_to_all x1, blocking collectives, body(): lax.all_to_all(reordered, 'tensor', split_axis=0, concat_axis=1, tiled=True)  192 us
    all_gather x1, waiting for transfers between devices, body(): piece = lax.all_gather(grad_out, 'tensor', axis=1, tiled=True)  113 us
    all_to_all x1, blocking collectives, body(): lax.all_to_all(kept, 'tensor', split_axis=1, concat_axis=0, tiled=True)  102 us
    unnamed x7, local copies, waits for them, and re-layouts  16.3 us
    dot_general x1, matrix products, body(): lax.dot_general(piece, acts, (((0,), (0,)), ((), ())), preferred_element_...  13.7 us
    dot_general x1, matrix products, body(): input_grad = jnp.dot(piece, columns, preferred_element_type=jnp.float32)  11.6 us
    mul x1, other arithmetic, body(): kept = weight * expand_mask(row_mask, side).astype(jnp.bfloat16)  10 us
  transfers between devices with their start and end apart: 2, of which 1 were waited for; matrix products, arithmetic and copies ran while one was open for 7% of the time, Pallas kernels for 0%

commit v1 on v0

--- a/solution.py
+++ b/solution.py
@@ -2,6 +2,26 @@
 import jax.numpy as jnp
 from jax import lax
 from jax.sharding import PartitionSpec as P
+from jax.lax import axis_index, axis_size, ppermute
+
+
+def get_sample(packet, dim_k):
+    last = list(packet.shape[1:])
+    last[dim_k] *= packet.shape[0]
+    return jnp.moveaxis(packet, 0, dim_k).reshape(last)
+
+
+def expand_samples_all_now(message, row_axis):
+    far_arr, odd = (axis_size(row_axis), axis_index(row_axis))
+    current_arr, local_part = (message[None], 1)
+    while local_part < far_arr:
+        v_now = ppermute(current_arr, row_axis, [(rr, rr ^ local_part) for rr in range(far_arr)])
+        r2 = odd & local_part == 0
+        current_arr = jnp.concatenate(
+            [jnp.where(r2, current_arr, v_now), jnp.where(r2, v_now, current_arr)]
+        )
+        local_part *= 2
+    return current_arr
 
 
 def expand_mask(mask, side):
@@ -22,7 +42,7 @@
     row_mask = lax.dynamic_slice_in_dim(block_mask, position * (d_tile // side), d_tile // side, 0)
     kept = weight * expand_mask(row_mask, side).astype(jnp.bfloat16)
     columns = lax.all_to_all(kept, "tensor", split_axis=1, concat_axis=0, tiled=True)
-    piece = lax.all_gather(grad_out, "tensor", axis=1, tiled=True)
+    piece = get_sample(expand_samples_all_now(grad_out, "tensor"), 1)
     input_grad = jnp.dot(piece, columns, preferred_element_type=jnp.float32)
     grad_rows = lax.dot_general(
         piece, acts, (((0,), (0,)), ((), ())), preferred_element_type=jnp.float32

time: 498 us -> 879 us (1.77)
  waiting for transfers between devices: 114 us -> 420 us
  local copies, waits for them, and re-layouts: 38.9 us -> 67.3 us
  other arithmetic: 11.6 us -> 39.4 us
  starting transfers between devices: 0.08 us -> 13.7 us
    ppermute x0 -> x6, waiting for transfers between devices: none -> 420 us  [expand_samples_all_now(): ppermute(current_arr, row_axis, [(rr, rr ^ local_part) for rr in range(fa...]
    all_gather x1 -> x0, waiting for transfers between devices: 113 us -> none  [body(): piece = lax.all_gather(grad_out, 'tensor', axis=1, tiled=True)]
    transpose x0 -> x1, local copies, waits for them, and re-layouts: none -> 22.4 us  [get_sample(): return jnp.moveaxis(packet, 0, dim_k).reshape(last)]
    select_n x0 -> x6, other arithmetic: none -> 15.4 us  [expand_samples_all_now(): jnp.where(r2, current_arr, v_now)]
    ppermute x0 -> x6, starting transfers between devices: none -> 13.7 us  [expand_samples_all_now(): ppermute(current_arr, row_axis, [(rr, rr ^ local_part) for rr in range(fa...]
    concatenate x0 -> x5, other arithmetic: none -> 11.3 us  [expand_samples_all_now(): jnp.concatenate([jnp.where(r2, current_arr, v_now), jnp.where(r2, v_now,...]
    unnamed x7 -> x18, local copies, waits for them, and re-layouts: 16.3 us -> 22.4 us
  transfers between devices with their start and end apart: 2 -> 7, of which waited for: 1 -> 6; matrix products, arithmetic and copies ran while one was open for 7% -> 3% of each run, Pallas kernels for 0% -> 0%
where the time goes in v1:
time: 879 us; the launch traced here: 878 us
  waiting for transfers between devices  420 us (48%)
  blocking collectives  301 us (34%)
  local copies, waits for them, and re-layouts  67.3 us (8%)
  other arithmetic  39.4 us (4%)
  matrix products  22.1 us (3%)
  between operations  14.2 us (2%)
  starting transfers between devices  13.7 us (2%)
    ppermute x6, waiting for transfers between devices, expand_samples_all_now(): ppermute(current_arr, row_axis, [(rr, rr ^ local_part) for rr in range(fa...  420 us
    all_to_all x1, blocking collectives, body(): lax.all_to_all(reordered, 'tensor', split_axis=0, concat_axis=1, tiled=True)  198 us
    all_to_all x1, blocking collectives, body(): lax.all_to_all(kept, 'tensor', split_axis=1, concat_axis=0, tiled=True)  102 us
    transpose x1, local copies, waits for them, and re-layouts, get_sample(): return jnp.moveaxis(packet, 0, dim_k).reshape(last)  22.4 us
    unnamed x18, local copies, waits for them, and re-layouts  22.4 us
  transfers between devices with their start and end apart: 7, of which 6 were waited for; matrix products, arithmetic and copies ran while one was open for 3% of the time, Pallas kernels for 0%

profile of v1, /device:TPU:1, one launch (start us, length us, event | category | flops | bytes accessed | tf_op | source)
XLA Modules:
  0.0 877.6 jit_solution(2927977418075962872)
XLA Ops:
  7.2 3.3 collective-permute-start
  10.6 1.4 collective-permute-done
  13.1 13.1 %collective-permute-done.1 = bf16[2,1024,128]{2,1,0:T(8,128)(2,1)S(1)} collective-permute-done((bf16[2,1024,128]{2,1,0:T(8,128)(2,1)S(1)}, bf16[2,1024,128]{2,1,0:T(8,128)(2,1)S(1)}, u32[]{:S(2)}, u32[]{:S(2)}) %collective-permute-start.1) | collective-permute-done | bytes 524320 | tf_op jit(solution)/shard_map/ppermute | solution.py:18
  26.3 1.1 pad_maximum_fusion.3
  27.3 1.6 collective-permute-start.2
  29.0 46.8 %collective-permute-done.2 = bf16[4,1024,128]{2,1,0:T(8,128)(2,1)S(1)} collective-permute-done((bf16[4,1024,128]{2,1,0:T(8,128)(2,1)}, bf16[4,1024,128]{2,1,0:T(8,128)(2,1)S(1)}, u32[]{:S(2)}, u32[]{:S(2)}) %collective-permute-start.2) | collective-permute-done | bytes 1048608 | tf_op jit(solution)/shard_map/ppermute | solution.py:18
  77.2 4.9 collective-permute-start.3
  82.1 90.9 %collective-permute-done.3 = bf16[8,1024,128]{2,1,0:T(8,128)(2,1)} collective-permute-done((bf16[8,1024,128]{2,1,0:T(8,128)(2,1)S(1)}, bf16[8,1024,128]{2,1,0:T(8,128)(2,1)}, u32[]{:S(2)}, u32[]{:S(2)}) %collective-permute-start.3) | collective-permute-done | bytes 2097184 | tf_op jit(solution)/shard_map/ppermute | solution.py:18
  173.0 2.4 broadcast_select_fusion.5
  175.5 2.6 pad_maximum_fusion.1
  178.1 1.1 collective-permute-start.4
  179.2 89.6 %collective-permute-done.4 = bf16[16,1024,128]{2,1,0:T(8,128)(2,1)} collective-permute-done((bf16[16,1024,128]{2,1,0:T(8,128)(2,1)}, bf16[16,1024,128]{2,1,0:T(8,128)(2,1)}, u32[]{:S(2)}, u32[]{:S(2)}) %collective-permute-start.4) | collective-permute-done | bytes 4194336 | tf_op jit(solution)/shard_map/ppermute | solution.py:18
  268.8 5.4 broadcast_select_fusion.3
  274.3 7.4 pad_maximum_fusion
  281.7 2.7 collective-permute-start.5
  284.4 178.4 %collective-permute-done.5 = bf16[32,1024,128]{2,1,0:T(8,128)(2,1)} collective-permute-done((bf16[32,1024,128]{2,1,0:T(8,128)(2,1)}, bf16[32,1024,128]{2,1,0:T(8,128)(2,1)}, u32[]{:S(2)}, u32[]{:S(2)}) %collective-permute-start.5) | collective-permute-done | bytes 8388640 | tf_op jit(solution)/shard_map/ppermute | solution.py:18
  462.9 6.3 broadcast_select_fusion.1
  469.2 3.2 copy-done.2
  472.4 2.5 copy-done.3
  474.9 6.7 maximum_bitcast_fusion
  481.7 22.4 %copy.18 = bf16[1024,64,128]{0,2,1:T(8,128)(2,1)} copy(bf16[1024,64,128]{2,0,1:T(8,128)(2,1)} %maximum_bitcast_fusion) | data formatting | bytes 33554432 | tf_op jit(solution)/shard_map/transpose | solution.py:11
  504.1 5.5 broadcast_in_dim.20
  509.5 13.1 %fusion = f32[8192,256]{1,0:T(8,128)S(1)} fusion(bf16[1024,8192]{0,1:T(8,128)(2,1)} %bitcast.36, bf16[1024,256]{1,0:T(8,128)(2,1)S(1)} %copy-done, f32[1024,8,2,128]{3,2,1,0:T(2,128)} %bitcast.37), kind=kOutput, calls=%fused_computation.2 | convolution fusion | flops 4299161600 | bytes 34078720 | tf_op jit(solution)/shard_map/dot_general | solution.py:47
  522.6 1.7 copy.19
  524.3 198.5 %all_to_all.35 = f32[64,128,256]{2,1,0:T(8,128)} all-to-all(f32[64,128,256]{2,1,0:T(8,128)S(1)} %bitcast.39), channel_id=1, replica_groups=mesh['dp'=4,'tensor'=64] {'tensor'}, dimensions={0} | all-to-all | bytes 16777216 | tf_op jit(solution)/shard_map/all_to_all | solution.py:61
  722.8 9.0 %copy.20 = f32[128,64,256]{0,2,1:T(8,128)} copy(f32[128,64,256]{2,0,1:T(8,128)} %bitcast.40) | data formatting | bytes 16777216 | tf_op jit(solution)/shard_map/all_to_all | solution.py:61
  731.7 9.0 %copy.22 = f32[128,16384]{1,0:T(8,128)} copy(f32[128,16384]{0,1:T(8,128)} %bitcast.41) | data formatting | bytes 16777216
  740.7 6.4 copy.16
  747.2 5.9 broadcast_multiply_fusion
  753.2 6.4 copy.17
  759.6 102.2 %all_to_all.36 = bf16[128,64,256]{2,0,1:T(8,128)(2,1)S(1)} all-to-all(bf16[128,64,256]{2,0,1:T(8,128)(2,1)} %copy.17), channel_id=1, replica_groups=mesh['dp'=4,'tensor'=64] {'tensor'}, dimensions={1} | all-to-all | bytes 8388608 | tf_op jit(solution)/shard_map/all_to_all | solution.py:44
  861.8 9.0 %fusion.6 = bf16[1024,256]{1,0:T(8,128)(2,1)} fusion(bf16[128,64,256]{2,0,1:T(8,128)(2,1)S(1)} %all_to_all.36, bf16[32,1024,128]{2,1,0:T(8,128)(2,1)} %copy-done.3, bf16[32,1024,128]{2,1,0:T(8,128)(2,1)} %copy-done.2), kind=kOutput, calls=%fused_computation.16 | convolution fusion | flops 4303618048 | bytes 21495808 | tf_op jit(solution)/shard_map/dot_general | solution.py:46
  (26 shorter events, 3.0 us)
Async XLA Ops:
  7.2 502.3 %copy-start = (bf16[1024,256]{1,0:T(8,128)(2,1)S(1)}, bf16[1024,256]{1,0:T(8,128)(2,1)}, u32[]{:S(2)}) copy-start(bf16[1024,256]{1,0:T(8,128)(2,1)} %param.5) | copy-start | bytes 1572868
  7.2 863.6 %reduce-scatter.4.cloned.1.call-start = ((), (), s32[]{:S(2)}) async-start(), calls=%async_computation.3 | async-start | bytes 10485760
  7.2 4.7 collective-permute-start
  13.0 13.2 %collective-permute-start.1 = (bf16[2,1024,128]{2,1,0:T(8,128)(2,1)S(1)}, bf16[2,1024,128]{2,1,0:T(8,128)(2,1)S(1)}, u32[]{:S(2)}, u32[]{:S(2)}) collective-permute-start(bf16[2,1024,128]{2,1,0:T(8,128)(2,1)S(1)} %pad_maximum_fusion.4), channel_id=1, source_target_pairs={{0,2},{1,3},{2,0},{3,1},{4,6},{5,7},{6,4},{7,5},{8,10},{9,11},{10,... | collective-permute-start | bytes 1572872 | tf_op jit(solution)/shard_map/ppermute | solution.py:18
  27.3 48.4 %collective-permute-start.2 = (bf16[4,1024,128]{2,1,0:T(8,128)(2,1)}, bf16[4,1024,128]{2,1,0:T(8,128)(2,1)S(1)}, u32[]{:S(2)}, u32[]{:S(2)}) collective-permute-start(bf16[4,1024,128]{2,1,0:T(8,128)(2,1)} %pad_maximum_fusion.3), channel_id=1, source_target_pairs={{0,4},{1,5},{2,6},{3,7},{4,0},{5,1},{6,2},{7,3},{8,12},{9,13},{10,... | collective-permute-start | bytes 3145736 | tf_op jit(solution)/shard_map/ppermute | solution.py:18
  75.9 1.0 copy-start.5
  75.9 1.3 copy-start.6
  77.2 95.8 %collective-permute-start.3 = (bf16[8,1024,128]{2,1,0:T(8,128)(2,1)S(1)}, bf16[8,1024,128]{2,1,0:T(8,128)(2,1)}, u32[]{:S(2)}, u32[]{:S(2)}) collective-permute-start(bf16[8,1024,128]{2,1,0:T(8,128)(2,1)S(1)} %pad_maximum_fusion.2), channel_id=1, source_target_pairs={{0,8},{1,9},{2,10},{3,11},{4,12},{5,13},{6,14},{7,15},{8,0},{9,1},... | collective-permute-start | bytes 6291464 | tf_op jit(solution)/shard_map/ppermute | solution.py:18
  175.4 2.7 copy-start.4
  178.1 90.7 %collective-permute-start.4 = (bf16[16,1024,128]{2,1,0:T(8,128)(2,1)}, bf16[16,1024,128]{2,1,0:T(8,128)(2,1)}, u32[]{:S(2)}, u32[]{:S(2)}) collective-permute-start(bf16[16,1024,128]{2,1,0:T(8,128)(2,1)} %pad_maximum_fusion.1), channel_id=1, source_target_pairs={{0,16},{1,17},{2,18},{3,19},{4,20},{5,21},{6,22},{7,23},{8,24},{9,... | collective-permute-start | bytes 12582920 | tf_op jit(solution)/shard_map/ppermute | solution.py:18
  274.3 10.1 %copy-start.7 = (s32[64,128]{1,0:T(8,128)S(1)}, s32[64,128]{1,0:T(8,128)}, u32[]{:S(2)}) copy-start(s32[64,128]{1,0:T(8,128)} %param.7) | copy-start | bytes 98308
  281.7 181.2 %collective-permute-start.5 = (bf16[32,1024,128]{2,1,0:T(8,128)(2,1)}, bf16[32,1024,128]{2,1,0:T(8,128)(2,1)}, u32[]{:S(2)}, u32[]{:S(2)}) collective-permute-start(bf16[32,1024,128]{2,1,0:T(8,128)(2,1)} %pad_maximum_fusion), channel_id=1, source_target_pairs={{0,32},{1,33},{2,34},{3,35},{4,36},{5,37},{6,38},{7,39},{8,40},{9,... | collective-permute-start | bytes 25165832 | tf_op jit(solution)/shard_map/ppermute | solution.py:18
  469.2 3.2 copy-start.2
  469.2 5.7 copy-start.3
  861.8 9.0 %copy-start.1 = (bf16[1024,256]{1,0:T(8,128)(2,1)S(1)}, bf16[1024,256]{1,0:T(8,128)(2,1)}, u32[]{:S(2)}) copy-start(bf16[1024,256]{1,0:T(8,128)(2,1)} %param.5) | copy-start | bytes 1572868
Sparse Core Ops, SparseCore 0:
  740.9 79.5 reduce-scatter.3
